TPU v7x, 256 devices: a whole 4x4x8 slice. The times are simulated.
256 devices in a mesh: row: 8 (over y, core), col: 32 (over x, z).
Axes of the slice: x: 4, y: 4, z: 8, core: 2. Of those that a mesh axis runs over, the one named last changes fastest.
Arguments:
- sources: float32 [65536, 256], P(('row', 'col')), may hold values from -6 to 6
- targets: float32 [65536, 256], P(('col', 'row')), may hold values from -6 to 6
- g_pot: float32 [65536], P(('col', 'row')), may hold values from -1 to 12
- log_a: float32 [65536], P(('row', 'col')), may hold values from -14 to -8
- log_b: float32 [65536], P(('col', 'row')), may hold values from -14 to -8
- src_block: int32 [16384], P(('row', 'col')), may hold values from 0 to 31, as said below
- tgt_block: int32 [16384], P(('row', 'col')), may hold values from 0 to 7, as said below
- pair_count: int32 [256], P(('row', 'col')), may hold values from 16 to 64, as said below
Outputs:
- f_new: float32 [65536], P(('row', 'col'))
- g_new: float32 [65536], P(('col', 'row'))
Inputs may be any that keep to these rules, and one draw needn't show every extreme that they name: `src_block`: within each row index, slot 0 of the 32 devices names together every source block of that row index once; slot k and slot k + 32 of a device name the same source block. `tgt_block`: within each col index, slot 0 of the 8 devices names together every target block of that col index once. `pair_count`: some device has all 64 slots live.
All inputs are finite; a program needn't handle non-finite values.
Results may differ from a plain program's by a relative error of at most 0.0003.
Values sent between devices are 32-bit elements; how exact they have to be, the bound alone decides.
A program may use at most 128 MiB of HBM per device.

v0:
```python
import jax
import jax.numpy as jnp
from jax import lax
from jax.sharding import PartitionSpec as P

BLK = 256
entropy = 0.05
lowest = -1e30


def squares_of(rows):
    return jnp.sum(rows * rows, axis=-1)


def cost_blocks(src_rows, tgt_rows, src_sq, tgt_sq):
    inner = jnp.einsum("kid,kjd->kij", src_rows, tgt_rows, precision=lax.Precision.HIGHEST)
    return (src_sq[:, :, None] + tgt_sq[:, None, :] - 2.0 * inner) / src_rows.shape[2]


def fold_blocks(slot_top, slot_total, slot_ids, alive, count):
    onehot = (slot_ids[:, None] == jnp.arange(count, dtype=jnp.int32)[None, :]) & alive[:, None]
    masked = jnp.where(onehot.T[:, :, None], slot_top[None, :, :], lowest)
    top = jnp.max(masked, axis=1)
    back = jnp.take(top, slot_ids, axis=0)
    weighted = jnp.where(alive[:, None], slot_total * jnp.exp(slot_top - back), 0.0)
    total = jnp.dot(onehot.T.astype(jnp.float32), weighted, precision=lax.Precision.HIGHEST)
    return (top.reshape(-1), total.reshape(-1))


def local(sources, targets, g_pot, log_a, log_b, src_block, tgt_block, pair_count):
    used_pairs = pair_count[0]
    slots = src_block.shape[0]
    alive = jnp.arange(slots, dtype=jnp.int32) < used_pairs
    tgt_all, pot_all = (
        lax.all_gather(targets, "row", axis=0, tiled=True),
        lax.all_gather(g_pot, "row", axis=0, tiled=True),
    )
    src_all, weight_all = (
        lax.all_gather(sources, "col", axis=0, tiled=True),
        lax.all_gather(log_a, "col", axis=0, tiled=True),
    )
    width = sources.shape[1]
    src_count = src_all.shape[0] // BLK
    tgt_count = tgt_all.shape[0] // BLK
    src_blocks = src_all.reshape(src_count, BLK, width)
    tgt_blocks = tgt_all.reshape(tgt_count, BLK, width)
    src_sq_all = squares_of(src_blocks)
    tgt_sq_all = squares_of(tgt_blocks)
    src_rows = jnp.take(src_blocks, src_block, axis=0)
    tgt_rows = jnp.take(tgt_blocks, tgt_block, axis=0)
    src_sq = jnp.take(src_sq_all, src_block, axis=0)
    tgt_sq = jnp.take(tgt_sq_all, tgt_block, axis=0)
    pot_rows = jnp.take(pot_all.reshape(tgt_count, BLK), tgt_block, axis=0)
    costs = cost_blocks(src_rows, tgt_rows, src_sq, tgt_sq)
    scores = (pot_rows[:, None, :] - costs) / entropy
    slot_top = jnp.max(scores, axis=2)
    slot_total = jnp.sum(jnp.exp(scores - slot_top[:, :, None]), axis=2)
    src_top, src_total = fold_blocks(slot_top, slot_total, src_block, alive, src_count)
    whole_top = lax.pmax(src_top, "col")
    src_total = lax.psum(src_total * jnp.exp(src_top - whole_top), "col")
    src_top = whole_top
    f_all = entropy * weight_all - entropy * (src_top + jnp.log(src_total))
    second_costs = cost_blocks(src_rows, tgt_rows, src_sq, tgt_sq)
    f_rows = jnp.take(f_all.reshape(src_count, BLK), src_block, axis=0)
    back_scores = (f_rows[:, :, None] - second_costs) / entropy
    col_top = jnp.max(back_scores, axis=1)
    col_total = jnp.sum(jnp.exp(back_scores - col_top[:, None, :]), axis=1)
    tgt_top, tgt_total = fold_blocks(col_top, col_total, tgt_block, alive, tgt_count)
    whole_tgt = lax.pmax(tgt_top, "row")
    tgt_total = lax.psum(tgt_total * jnp.exp(tgt_top - whole_tgt), "row")
    tgt_top = whole_tgt
    own_src = sources.shape[0]
    own_tgt = targets.shape[0]
    f_own = lax.dynamic_slice_in_dim(f_all, lax.axis_index("col") * own_src, own_src, 0)
    tgt_offset = lax.axis_index("row") * own_tgt
    top_own = lax.dynamic_slice_in_dim(tgt_top, tgt_offset, own_tgt, 0)
    total_own = lax.dynamic_slice_in_dim(tgt_total, tgt_offset, own_tgt, 0)
    g_own = entropy * log_b - entropy * (top_own + jnp.log(total_own))
    return (f_own, g_own)


def solution(mesh):
    placed = (
        P(("row", "col"), None),
        P(("col", "row"), None),
        P(("col", "row")),
        P(("row", "col")),
        P(("col", "row")),
        P(("row", "col")),
        P(("row", "col")),
        P(("row", "col")),
    )
    return jax.shard_map(
        local,
        mesh=mesh,
        in_specs=placed,
        out_specs=(P(("row", "col")), P(("col", "row"))),
        check_vma=False,
    )
```

profile of v0, /device:TPU:1, one launch (start us, length us, event | category | flops | bytes accessed | tf_op | source)
XLA Modules:
  0.0 527.1 jit_solution(1191801241612126786)
XLA Ops:
  7.2 0.0 all-gather.7.cloned.1.call-start
  7.2 0.7 all-gather.7.cloned.1.call-update
  7.9 0.0 all-gather.5.cloned.1.call-start
  7.9 0.7 all-gather.5.cloned.1.call-update
  8.7 12.4 %all-gather.1 = f32[8,1,256]{2,1,0:T(1,128)S(1)} all-gather(f32[1,1,256]{2,1,0:T(1,128)} %bitcast.32), channel_id=1, replica_groups=mesh['row'=8,'col'=32] {'row'}, dimensions={0}, use_global_device_ids=true | all-gather | bytes 9216 | tf_op jit(solution)/shard_map/all_gather | solution.py:36
  21.7 0.7 compare_select_fusion.1
  22.4 0.7 gather_fusion.2
  23.0 37.7 %all-gather = f32[32,1,256]{2,1,0:T(1,128)S(1)} all-gather(f32[1,1,256]{2,1,0:T(1,128)} %bitcast.33), channel_id=1, replica_groups=mesh['row'=8,'col'=32] {'col'}, dimensions={0}, use_global_device_ids=true | all-gather | bytes 33792 | tf_op jit(solution)/shard_map/all_gather | solution.py:40
  60.8 0.7 compare_select_fusion
  61.4 0.7 compare_and_fusion.1
  62.1 0.7 compare_and_fusion
  62.8 0.7 fusion.37
  63.4 0.7 fusion.36
  64.1 0.0 all-gather.7.cloned.1.call-done
  64.2 1.9 multiply_reduce_fusion.1
  66.1 0.7 gather_fusion.4
  66.8 10.5 %gather_fusion.1 = f32[64,256,256]{2,1,0:T(8,128)} fusion(f32[8,256,256]{2,1,0:T(8,128)} %bitcast.20, s32[1024]{0:T(1024)S(1)} %pad_clamp_fusion.1), kind=kCustom, calls=%fused_computation.7 | custom fusion | bytes 33554688 | tf_op jit(solution)/shard_map/jit(_take)/gather | solution.py:50
  77.3 0.1 broadcast_select_fusion.3
  77.3 64.3 %all-gather.5.cloned.1.call-done = f32[8192,256]{1,0:T(8,128)} async-done(((f32[256,256]{1,0:T(8,128)}), f32[8192,256]{1,0:T(8,128)}) %all-gather.5.cloned.1.call-update) | async-done | bytes 8388624 | tf_op jit(solution)/shard_map/all_gather | solution.py:39
  141.6 4.5 multiply_reduce_fusion
  146.2 0.7 gather_fusion.3
  146.8 11.6 %gather_fusion = f32[64,256,256]{2,1,0:T(8,128)} fusion(f32[32,256,256]{2,1,0:T(8,128)} %bitcast.21, s32[1024]{0:T(1024)S(1)} %pad_clamp_fusion), kind=kCustom, calls=%fused_computation.6 | custom fusion | bytes 33554688 | tf_op jit(solution)/shard_map/jit(_take)/gather | solution.py:49
  158.5 0.1 broadcast_select_fusion.2
  158.5 29.9 %fusion.3 = (f32[64,256]{1,0:T(8,128)S(1)}, f32[64,256,256]{2,1,0:T(8,128)}) fusion(f32[64,256]{1,0:T(8,128)S(1)} %get-tuple-element.4, f32[64,256,256]{2,1,0:T(8,128)} %gather_fusion.1, pred[64]{0:T(512)(128)(4,1)S(1)} %compare_and_fusion.1, f32[64,256,256]{2,1,0:T(8,128)} %gather_fusion, pred[64]{0:T(512)(128)(4,1)S(1)} %compare_and_fusion, ...), kind=kOutput, calls=%fused_computation.16 | convolution fusion | flops 12922634240 | bytes 50593920 | tf_op jit(solution)/shard_map/kid,kjd->kij/dot_general | solution.py:16
  188.4 0.0 copy-start.1
  188.4 8.5 %exponential_reduce_fusion.1 = f32[64,256]{1,0:T(8,128)S(1)} fusion(f32[64,256,256]{2,1,0:T(8,128)} %get-tuple-element.7, f32[64,256]{1,0:T(8,128)S(1)} %get-tuple-element.6, f32[64,256]{1,0:T(8,128)S(1)} %get-tuple-element.4), kind=kLoop, calls=%fused_computation.10 | loop fusion | flops 16760832 | bytes 16973824 | tf_op jit(solution)/shard_map/reduce_sum | solution.py:57
  197.0 0.5 select_reduce_fusion
  197.5 0.7 gather_fusion.5
  198.2 0.0 copy-done.1
  198.2 0.3 convolution_bitcast_fusion
  198.5 111.5 %pmax.14 = f32[8192]{0:T(1024)S(1)} all-reduce(f32[8192]{0:T(1024)S(1)} %bitcast.25), channel_id=1, replica_groups=mesh['row'=8,'col'=32] {'col'}, use_global_device_ids=true, to_apply=%region_4.7 | all-reduce | flops 8192 | bytes 65536 | tf_op jit(solution)/shard_map/pmax | solution.py:59
  310.0 110.7 %psum.14 = f32[8192]{0:T(1024)S(1)} all-reduce(f32[8192]{0:T(1024)S(1)} %exponential_multiply_fusion), channel_id=1, replica_groups=mesh['row'=8,'col'=32] {'col'}, use_global_device_ids=true, to_apply=%region_6.9 | all-reduce | flops 8192 | bytes 65536 | tf_op jit(solution)/shard_map/psum | solution.py:60
  420.8 0.7 gather_fusion.6
  421.4 0.1 broadcast_select_fusion
  421.5 0.0 copy-start.2
  421.5 0.0 copy-start
  421.5 7.2 %fusion.4 = f32[64,256]{1,0:T(8,128)S(1)} fusion(f32[64,256,256]{2,1,0:T(8,128)} %get-tuple-element.7, f32[64,256]{1,0:T(8,128)S(1)} %broadcast_select_fusion), kind=kLoop, calls=%fused_computation.17 | loop fusion | flops 12566528 | bytes 16908288 | tf_op jit(solution)/shard_map/reduce_max | solution.py:66
  428.8 8.0 %exponential_reduce_fusion = f32[64,256]{1,0:T(8,128)S(1)} fusion(f32[64,256,256]{2,1,0:T(8,128)} %get-tuple-element.7, f32[64,256]{1,0:T(8,128)S(1)} %fusion.4, f32[64,256]{1,0:T(8,128)S(1)} %broadcast_select_fusion), kind=kLoop, calls=%fused_computation.8 | loop fusion | flops 16760832 | bytes 16973824 | tf_op jit(solution)/shard_map/reduce_sum | solution.py:67
  436.8 0.1 select_reduce_fusion.1
  437.0 0.7 gather_fusion.7
  437.6 0.0 copy-done.2
  437.6 0.3 convolution_bitcast_fusion.1
  437.9 68.4 %pmax.15 = f32[2048]{0:T(1024)S(1)} all-reduce(f32[2048]{0:T(1024)S(1)} %bitcast.29), channel_id=1, replica_groups=mesh['row'=8,'col'=32] {'row'}, use_global_device_ids=true, to_apply=%region_9.12 | all-reduce | flops 2048 | bytes 16384 | tf_op jit(solution)/shard_map/pmax | solution.py:69
  506.3 12.7 %psum.15 = f32[2048]{0:T(1024)S(1)} all-reduce(f32[2048]{0:T(1024)S(1)} %exponential_multiply_fusion.1), channel_id=1, replica_groups=mesh['row'=8,'col'=32] {'row'}, use_global_device_ids=true, to_apply=%region_11.14 | all-reduce | flops 2048 | bytes 16384 | tf_op jit(solution)/shard_map/psum | solution.py:70
  519.0 0.6 dynamic_slice.9
  519.7 0.0 copy-done
  519.7 0.6 multiply_subtract_fusion.1
  (15 shorter events, 0.2 us)
Async XLA Ops:
  7.2 57.0 %all-gather.7.cloned.1.call-start = ((), (), s32[]{:S(2)}) async-start(), calls=%async_computation.1 | async-start | bytes 2359296 | tf_op jit(solution)/shard_map/all_gather | solution.py:35
  7.9 133.7 %all-gather.5.cloned.1.call-start = ((), (), s32[]{:S(2)}) async-start(), calls=%async_computation | async-start | bytes 8650752 | tf_op jit(solution)/shard_map/all_gather | solution.py:39
  188.4 9.7 %copy-start.1 = (s32[64]{0:T(128)S(1)}, s32[64]{0:T(128)}, u32[]{:S(2)}) copy-start(s32[64]{0:T(128)} %param.17) | copy-start | bytes 772
  421.5 16.1 %copy-start.2 = (s32[64]{0:T(128)S(1)}, s32[64]{0:T(128)}, u32[]{:S(2)}) copy-start(s32[64]{0:T(128)} %param.18) | copy-start | bytes 772
  421.5 98.1 %copy-start = (f32[256]{0:T(256)S(1)}, f32[256]{0:T(256)}, u32[]{:S(2)}) copy-start(f32[256]{0:T(256)} %param.16) | copy-start | bytes 3076
Sparse Core Ops, SparseCore 0:
  9.8 32.0 all-gather.6
  44.5 97.0 all-gather.4
where the time goes:
time: 528 us; the launch traced here: 527 us
  blocking collectives  353 us (67%)
  waiting for transfers between devices  65.7 us (12%)
  other arithmetic  35.9 us (7%)
  matrix products  30.4 us (6%)
  local copies, waits for them, and re-layouts  26.8 us (5%)
  between operations  14.9 us (3%)
    pmax x1, blocking collectives, local(): whole_top = lax.pmax(src_top, 'col')  112 us
    psum x1, blocking collectives, local(): src_total = lax.psum(src_total * jnp.exp(src_top - whole_top), 'col')  111 us
    pmax x1, blocking collectives, local(): whole_tgt = lax.pmax(tgt_top, 'row')  68.4 us
    all_gather x1, waiting for transfers between devices, local(): lax.all_gather(sources, 'col', axis=0, tiled=True)  64.3 us
    all_gather x1, blocking collectives, local(): lax.all_gather(log_a, 'col', axis=0, tiled=True)  37.7 us
    dot_general x1, matrix products, cost_blocks(): jnp.einsum('kid,kjd->kij', src_rows, tgt_rows, precision=lax.Precision.HI...  29.9 us
    psum x1, blocking collectives, local(): tgt_total = lax.psum(tgt_total * jnp.exp(tgt_top - whole_tgt), 'row')  12.7 us
    all_gather x1, blocking collectives, local(): lax.all_gather(g_pot, 'row', axis=0, tiled=True)  12.4 us
  transfers between devices with their start and end apart: 2, of which 1 were waited for; matrix products, arithmetic and copies ran while one was open for 3% of the time, Pallas kernels for 0%

commit v1 on v0

--- a/solution.py
+++ b/solution.py
@@ -57,7 +57,9 @@
     slot_total = jnp.sum(jnp.exp(scores - slot_top[:, :, None]), axis=2)
     src_top, src_total = fold_blocks(slot_top, slot_total, src_block, alive, src_count)
     whole_top = lax.pmax(src_top, "col")
-    src_total = lax.psum(src_total * jnp.exp(src_top - whole_top), "col")
+    own = src_total * jnp.exp(src_top - whole_top)
+    parts = lax.all_gather(own, "col", axis=0, tiled=False)
+    src_total = parts.sum(axis=0)
     src_top = whole_top
     f_all = entropy * weight_all - entropy * (src_top + jnp.log(src_total))
     second_costs = cost_blocks(src_rows, tgt_rows, src_sq, tgt_sq)

time: 528 us -> 462 us (0.88)
  blocking collectives: 353 us -> 186 us
  waiting for transfers between devices: 65.7 us -> 167 us
    psum x1 -> x0, blocking collectives: 111 us -> none  [local(): src_total = lax.psum(src_total * jnp.exp(src_top - whole_top), 'col')]
    all_gather x0 -> x1, waiting for transfers between devices: none -> 62.3 us  [local(): parts = lax.all_gather(own, 'col', axis=0, tiled=False)]
    pmax x1, blocking collectives: 68.4 us -> 17.7 us  [local(): whole_tgt = lax.pmax(tgt_top, 'row')]
    all_gather x1, waiting for transfers between devices: 64.3 us -> 86.6 us  [local(): lax.all_gather(sources, 'col', axis=0, tiled=True)]
    all_gather x1, waiting for transfers between devices: 0.02 us -> 16.2 us  [local(): lax.all_gather(targets, 'row', axis=0, tiled=True)]
    all_gather x1, blocking collectives: 37.7 us -> 31.2 us  [local(): lax.all_gather(log_a, 'col', axis=0, tiled=True)]
  transfers between devices with their start and end apart: 2 -> 3, of which waited for: 1 -> 3; matrix products, arithmetic and copies ran while one was open for 3% -> 4% of each run, Pallas kernels for 0% -> 0%
where the time goes in v1:
time: 462 us; the launch traced here: 461 us
  blocking collectives  186 us (40%)
  waiting for transfers between devices  167 us (36%)
  other arithmetic  35.9 us (8%)
  matrix products  30.5 us (7%)
  local copies, waits for them, and re-layouts  28.1 us (6%)
  between operations  14.6 us (3%)
    pmax x1, blocking collectives, local(): whole_top = lax.pmax(src_top, 'col')  112 us
    all_gather x1, waiting for transfers between devices, local(): lax.all_gather(sources, 'col', axis=0, tiled=True)  86.6 us
    all_gather x1, waiting for transfers between devices, local(): parts = lax.all_gather(own, 'col', axis=0, tiled=False)  62.3 us
    all_gather x1, blocking collectives, local(): lax.all_gather(log_a, 'col', axis=0, tiled=True)  31.2 us
    dot_general x1, matrix products, cost_blocks(): jnp.einsum('kid,kjd->kij', src_rows, tgt_rows, precision=lax.Precision.HI...  29.9 us
    pmax x1, blocking collectives, local(): whole_tgt = lax.pmax(tgt_top, 'row')  17.7 us
    all_gather x1, waiting for transfers between devices, local(): lax.all_gather(targets, 'row', axis=0, tiled=True)  16.2 us
    psum x1, blocking collectives, local(): tgt_total = lax.psum(tgt_total * jnp.exp(tgt_top - whole_tgt), 'row')  12.7 us
  transfers between devices with their start and end apart: 3, of which 3 were waited for; matrix products, arithmetic and copies ran while one was open for 4% of the time, Pallas kernels for 0%

profile of v1, /device:TPU:1, one launch (start us, length us, event | category | flops | bytes accessed | tf_op | source)
XLA Modules:
  0.0 461.3 jit_solution(2991369276296060857)
XLA Ops:
  7.2 0.0 all-gather.9.cloned.1.call-start
  7.2 0.7 all-gather.9.cloned.1.call-update
  7.9 0.0 all-gather.7.cloned.1.call-start
  7.9 0.7 all-gather.7.cloned.1.call-update
  8.6 0.0 all-gather.11.cloned.1.call-start
  8.7 12.4 %all-gather.2 = f32[8,1,256]{2,1,0:T(1,128)S(1)} all-gather(f32[1,1,256]{2,1,0:T(1,128)} %bitcast.32), channel_id=1, replica_groups=mesh['row'=8,'col'=32] {'row'}, dimensions={0}, use_global_device_ids=true | all-gather | bytes 9216 | tf_op jit(solution)/shard_map/all_gather | solution.py:36
  21.7 0.7 compare_select_fusion.1
  22.4 0.7 gather_fusion.2
  23.1 0.7 compare_select_fusion
  23.7 0.7 compare_and_fusion.1
  24.4 0.7 compare_and_fusion
  25.1 0.7 fusion.36
  25.7 16.2 %all-gather.9.cloned.1.call-done = f32[2048,256]{1,0:T(8,128)} async-done(((f32[256,256]{1,0:T(8,128)}), f32[2048,256]{1,0:T(8,128)}) %all-gather.9.cloned.1.call-update) | async-done | bytes 2097168 | tf_op jit(solution)/shard_map/all_gather | solution.py:35
  41.9 1.9 multiply_reduce_fusion.1
  43.9 0.7 gather_fusion.4
  44.5 10.4 %gather_fusion.1 = f32[64,256,256]{2,1,0:T(8,128)} fusion(f32[8,256,256]{2,1,0:T(8,128)} %bitcast.20, s32[1024]{0:T(1024)S(1)} %pad_clamp_fusion.1), kind=kCustom, calls=%fused_computation.7 | custom fusion | bytes 33554688 | tf_op jit(solution)/shard_map/jit(_take)/gather | solution.py:50
  54.9 0.1 broadcast_select_fusion.3
  55.0 86.6 %all-gather.7.cloned.1.call-done = f32[8192,256]{1,0:T(8,128)} async-done(((f32[256,256]{1,0:T(8,128)}), f32[8192,256]{1,0:T(8,128)}) %all-gather.7.cloned.1.call-update) | async-done | bytes 8388624 | tf_op jit(solution)/shard_map/all_gather | solution.py:39
  141.6 4.5 multiply_reduce_fusion
  146.2 0.7 gather_fusion.3
  146.8 11.6 %gather_fusion = f32[64,256,256]{2,1,0:T(8,128)} fusion(f32[32,256,256]{2,1,0:T(8,128)} %bitcast.21, s32[1024]{0:T(1024)S(1)} %pad_clamp_fusion), kind=kCustom, calls=%fused_computation.6 | custom fusion | bytes 33554688 | tf_op jit(solution)/shard_map/jit(_take)/gather | solution.py:49
  158.5 0.1 broadcast_select_fusion.2
  158.5 29.9 %fusion.3 = (f32[64,256]{1,0:T(8,128)S(1)}, f32[64,256,256]{2,1,0:T(8,128)}) fusion(f32[64,256]{1,0:T(8,128)S(1)} %get-tuple-element.4, f32[64,256,256]{2,1,0:T(8,128)} %gather_fusion.1, pred[64]{0:T(512)(128)(4,1)S(1)} %compare_and_fusion.1, f32[64,256,256]{2,1,0:T(8,128)} %gather_fusion, pred[64]{0:T(512)(128)(4,1)S(1)} %compare_and_fusion, ...), kind=kOutput, calls=%fused_computation.16 | convolution fusion | flops 12922634240 | bytes 50593920 | tf_op jit(solution)/shard_map/kid,kjd->kij/dot_general | solution.py:16
  188.5 8.6 %exponential_reduce_fusion.1 = f32[64,256]{1,0:T(8,128)S(1)} fusion(f32[64,256,256]{2,1,0:T(8,128)} %get-tuple-element.7, f32[64,256]{1,0:T(8,128)S(1)} %get-tuple-element.6, f32[64,256]{1,0:T(8,128)S(1)} %get-tuple-element.4), kind=kLoop, calls=%fused_computation.10 | loop fusion | flops 16760832 | bytes 16973824 | tf_op jit(solution)/shard_map/reduce_sum | solution.py:57
  197.0 0.5 select_reduce_fusion
  197.5 0.7 gather_fusion.5
  198.2 0.0 copy-done.2
  198.2 0.3 convolution_bitcast_fusion
  198.6 111.5 %pmax.14 = f32[8192]{0:T(1024)S(1)} all-reduce(f32[8192]{0:T(1024)S(1)} %bitcast.25), channel_id=1, replica_groups=mesh['row'=8,'col'=32] {'col'}, use_global_device_ids=true, to_apply=%region_4.7 | all-reduce | flops 8192 | bytes 65536 | tf_op jit(solution)/shard_map/pmax | solution.py:59
  310.1 0.6 exponential_multiply_fusion
  310.7 0.0 all-gather.11.cloned.1.call-update
  310.7 0.0 copy-done
  310.7 31.2 %all-gather.1 = f32[32,1,256]{2,1,0:T(1,128)S(1)} all-gather(f32[1,1,256]{2,1,0:T(1,128)S(1)} %bitcast.33), channel_id=1, replica_groups=mesh['row'=8,'col'=32] {'col'}, dimensions={0}, use_global_device_ids=true | all-gather | bytes 33792 | tf_op jit(solution)/shard_map/all_gather | solution.py:40
  342.0 62.3 %all-gather.11.cloned.1.call-done = f32[262144]{0:T(1024)} async-done(((f32[8192]{0:T(1024)}), f32[262144]{0:T(1024)}) %all-gather.11.cloned.1.call-update) | async-done | bytes 1048592 | tf_op jit(solution)/shard_map/all_gather | solution.py:61
  404.3 1.4 reshape.194
  405.7 0.1 reduce_sum.54
  405.9 0.7 gather_fusion.6
  406.5 0.1 broadcast_select_fusion
  406.6 0.0 copy-start.1
  406.6 7.2 %fusion.4 = f32[64,256]{1,0:T(8,128)S(1)} fusion(f32[64,256,256]{2,1,0:T(8,128)} %get-tuple-element.7, f32[64,256]{1,0:T(8,128)S(1)} %broadcast_select_fusion), kind=kLoop, calls=%fused_computation.17 | loop fusion | flops 12566528 | bytes 16908288 | tf_op jit(solution)/shard_map/reduce_max | solution.py:68
  413.9 8.0 %exponential_reduce_fusion = f32[64,256]{1,0:T(8,128)S(1)} fusion(f32[64,256,256]{2,1,0:T(8,128)} %get-tuple-element.7, f32[64,256]{1,0:T(8,128)S(1)} %fusion.4, f32[64,256]{1,0:T(8,128)S(1)} %broadcast_select_fusion), kind=kLoop, calls=%fused_computation.8 | loop fusion | flops 16760832 | bytes 16973824 | tf_op jit(solution)/shard_map/reduce_sum | solution.py:69
  421.9 0.1 select_reduce_fusion.1
  422.1 0.7 gather_fusion.7
  422.7 0.3 convolution_bitcast_fusion.1
  423.0 17.7 %pmax.15 = f32[2048]{0:T(1024)S(1)} all-reduce(f32[2048]{0:T(1024)S(1)} %bitcast.29), channel_id=1, replica_groups=mesh['row'=8,'col'=32] {'row'}, use_global_device_ids=true, to_apply=%region_9.12 | all-reduce | flops 2048 | bytes 16384 | tf_op jit(solution)/shard_map/pmax | solution.py:71
  440.8 12.7 %psum.7 = f32[2048]{0:T(1024)S(1)} all-reduce(f32[2048]{0:T(1024)S(1)} %exponential_multiply_fusion.1), channel_id=1, replica_groups=mesh['row'=8,'col'=32] {'row'}, use_global_device_ids=true, to_apply=%region_11.14 | all-reduce | flops 2048 | bytes 16384 | tf_op jit(solution)/shard_map/psum | solution.py:72
  453.4 0.6 dynamic_slice.9
  454.1 0.6 multiply_subtract_fusion.1
  (20 shorter events, 0.2 us)
Async XLA Ops:
  7.2 34.8 %all-gather.9.cloned.1.call-start = ((), (), s32[]{:S(2)}) async-start(), calls=%async_computation.1 | async-start | bytes 2359296 | tf_op jit(solution)/shard_map/all_gather | solution.py:35
  7.9 133.7 %all-gather.7.cloned.1.call-start = ((), (), s32[]{:S(2)}) async-start(), calls=%async_computation | async-start | bytes 8650752 | tf_op jit(solution)/shard_map/all_gather | solution.py:39
  8.6 395.7 %all-gather.11.cloned.1.call-start = ((), (), s32[]{:S(2)}) async-start(), calls=%async_computation.2 | async-start | bytes 1081344 | tf_op jit(solution)/shard_map/all_gather | solution.py:61
  188.4 9.8 %copy-start.2 = (s32[64]{0:T(128)S(1)}, s32[64]{0:T(128)}, u32[]{:S(2)}) copy-start(s32[64]{0:T(128)} %param.17) | copy-start | bytes 772
  188.4 122.3 %copy-start = (f32[256]{0:T(256)S(1)}, f32[256]{0:T(256)}, u32[]{:S(2)}) copy-start(f32[256]{0:T(256)} %param.15) | copy-start | bytes 3076
  188.4 153.5 %copy-start.3 = (s32[64]{0:T(128)S(1)}, s32[64]{0:T(128)}, u32[]{:S(2)}) copy-start(s32[64]{0:T(128)} %param.18) | copy-start | bytes 772
  406.6 47.5 %copy-start.1 = (f32[256]{0:T(256)S(1)}, f32[256]{0:T(256)}, u32[]{:S(2)}) copy-start(f32[256]{0:T(256)} %param.16) | copy-start | bytes 3076
Sparse Core Ops, SparseCore 0:
  9.8 32.0 all-gather.8
  44.5 97.0 all-gather.6
  310.8 93.4 all-gather.10
